TPU v7x, 256 devices: a whole 4x4x8 slice. The times are simulated.
256 devices in a mesh: tm: 8 (over x, y_lo), pts: 32 (over y_hi, z, core).
Axes of the slice: x: 4, y: 4 (y_hi: 2, y_lo: 2; y = y_hi * 2 + y_lo), z: 8, core: 2. Of those that a mesh axis runs over, the one named last changes fastest.
Arguments:
- orbitals: bfloat16 [32768, 2048], P('pts'), may hold values from -6 to 6
- panel_orbitals: bfloat16 [1024, 2048], P(('tm', 'pts')), may hold values from -0.1796875 to 0.1796875
- band_gap: float32 [2048], replicated, may hold values from 0.1 to 1
- tau_points: float32 [8], replicated, may hold values from 0.1 to 2
- quad_weight: float32 [8], replicated, may hold values from 0.1 to 1
- frequencies: float32 [8], replicated, may hold values from 0.1 to 3
- coulomb: bfloat16 [1024, 1024], P(('tm', 'pts')), may hold values from -0.1875 to 0.1875
Outputs:
- screened: bfloat16 [8, 32768, 1024], P(None, ('pts', 'tm'))
All inputs are finite; a program needn't handle non-finite values.
Results may differ from a plain program's by a relative error of at most 0.0056.
Values may be sent and summed in bfloat16 or wider, within the bound.
No kernel may reach another device: no remote copies, remote signals or barrier semaphores. Data moves between devices by JAX's collectives and lax.ppermute only.
A program may use at most 64 MiB of HBM per device.

v0:
```python
import jax
import jax.numpy as jnp
from jax import lax
from jax.sharding import PartitionSpec as P

NOCC = 512
PANEL = 1024
TAU_DEV = 1
FREQS = 8


def laid_out(pieces, dim):
    lengths = list(pieces.shape[1:])
    lengths[dim] *= pieces.shape[0]
    return jnp.moveaxis(pieces, 0, dim).reshape(lengths)


def sent_to_all(value, axis):
    copies = jnp.broadcast_to(value, (lax.axis_size(axis), *value.shape))
    return lax.all_to_all(copies, axis, split_axis=0, concat_axis=0, tiled=True)


def gather_directly(value, axis, dim):
    return laid_out(sent_to_all(value, axis), dim)


def in_blocks(value, dim, devices):
    before, after = (value.shape[:dim], value.shape[dim + 1 :])
    return jnp.moveaxis(value.reshape(*before, devices, -1, *after), dim, 0)


def cut_rows(length, count):
    lap = length // count
    if lap >= 8:
        lap -= lap % 8
    return [lap * k for k in range(1, count)]


def several_exchanges(value, axis, pieces, split_dim, concat_dim):
    blocks = in_blocks(value, split_dim, lax.axis_size(axis))
    cut = max(range(1, max(2, blocks.ndim - 1)), key=lambda d: blocks.shape[d])
    gathered = []
    for section in jnp.split(blocks, cut_rows(blocks.shape[cut], pieces), axis=cut):
        if section.size:
            gathered.append(lax.all_to_all(section, axis, split_axis=0, concat_axis=0, tiled=True))
    return laid_out(jnp.concatenate(gathered, axis=cut), concat_dim)


def contract(left, right):
    return lax.dot_general(
        left, right, (((1,), (1,)), ((), ())), preferred_element_type=jnp.float32
    )


def shards(orbitals, panel_orbitals, band_gap, tau_points, quad_weight, frequencies, coulomb):
    group = lax.axis_index("tm")
    own_taus = lax.dynamic_slice_in_dim(tau_points, group * TAU_DEV, TAU_DEV)
    decay = jnp.exp(-band_gap[None, :] * own_taus[:, None])
    occ_rows = orbitals[:, :NOCC]
    vir_rows = orbitals[:, NOCC:]
    grouped = gather_directly(panel_orbitals, "pts", 0)
    widened = lax.all_gather(grouped, "tm", axis=0, tiled=True).astype(jnp.float32)
    scaled = (widened * decay[0][None, :]).astype(jnp.bfloat16)
    green_occ = contract(occ_rows, scaled[:, :NOCC])
    green_vir = contract(vir_rows, scaled[:, NOCC:])
    layers = [(-(green_occ * green_vir)).astype(jnp.bfloat16)]
    polar = jnp.stack(layers)
    regrouped = several_exchanges(polar, "tm", 2, 1, 0)
    times_all = regrouped.shape[0]
    row_count = regrouped.shape[1]
    cosines = quad_weight[None, :] * jnp.cos(frequencies[:, None] * tau_points[None, :])
    flat = regrouped.reshape(times_all, row_count * PANEL).astype(jnp.float32)
    transformed = jnp.dot(cosines, flat, precision=lax.Precision.HIGHEST).astype(jnp.bfloat16)
    transformed = transformed.reshape(FREQS * row_count, PANEL)
    screened = jnp.dot(
        transformed,
        lax.all_gather(coulomb, ("tm", "pts"), axis=0, tiled=True),
        preferred_element_type=jnp.float32,
    )
    return screened.astype(jnp.bfloat16).reshape(FREQS, row_count, PANEL)


def solution(mesh):
    placed = (P("pts", None), P(("tm", "pts"), None), P(), P(), P(), P(), P(("tm", "pts"), None))
    return jax.shard_map(
        shards, mesh=mesh, in_specs=placed, out_specs=P(None, ("pts", "tm"), None), check_vma=False
    )
```

profile of v0, /device:TPU:98, one launch (start us, length us, event | category | flops | bytes accessed | tf_op | source)
XLA Modules:
  0.0 566.2 jit_solution(4525019650464051369)
XLA Ops:
  6.5 0.0 copy-start.2
  6.5 0.0 all-gather.4.cloned.1.call-start
  6.5 1.0 broadcast_in_dim.2
  7.5 27.3 %all_to_all.15 = bf16[32,4,2048]{2,1,0:T(4,128)(2,1)S(1)} all-to-all(bf16[32,4,2048]{2,1,0:T(4,128)(2,1)S(1)} %broadcast_in_dim.2), channel_id=1, replica_groups=mesh['tm'=8,'pts'=32] {'pts'}, dimensions={0} | all-to-all | bytes 1048576 | tf_op jit(solution)/shard_map/all_to_all | solution.py:20
  34.9 0.9 reshape.19
  35.8 0.0 all-gather.4.cloned.1.call-update
  35.8 0.0 all-gather.6.cloned.1.call-start
  35.8 0.7 all-gather.6.cloned.1.call-update
  36.5 0.0 copy-done.2
  36.6 0.7 dynamic_slice.3
  37.2 0.0 copy-done.1
  37.2 0.7 multiply_exponential_fusion
  37.9 87.4 %all-gather.4.cloned.1.call-done = bf16[1024,2048]{1,0:T(8,128)(2,1)} async-done(((bf16[128,2048]{1,0:T(8,128)(2,1)}), bf16[1024,2048]{1,0:T(8,128)(2,1)}) %all-gather.4.cloned.1.call-update) | async-done | bytes 4194320 | tf_op jit(solution)/shard_map/all_gather | solution.py:62
  125.4 3.4 multiply_convert_fusion
  128.8 0.0 copy-done
  128.8 3.4 fusion
  132.3 1.3 negate_convert_fusion
  133.6 1.2 fusion.11
  134.8 20.0 %all_to_all.16 = bf16[8,1,64,1024]{3,2,1,0:T(8,128)(2,1)S(1)} all-to-all(bf16[8,1,64,1024]{3,2,1,0:T(8,128)(2,1)S(1)} %get-tuple-element.5), channel_id=1, replica_groups=mesh['tm'=8,'pts'=32] {'tm'}, dimensions={0} | all-to-all | bytes 2097152 | tf_op jit(solution)/shard_map/all_to_all | solution.py:45
  154.8 4.8 all-to-all-start.2
  159.6 384.3 %all-gather.6.cloned.1.call-done = bf16[256,4,1024]{2,1,0:T(4,128)(2,1)} async-done(((bf16[1,4,1024]{2,1,0:T(4,128)(2,1)}), bf16[256,4,1024]{2,1,0:T(4,128)(2,1)}) %all-gather.6.cloned.1.call-update) | async-done | bytes 2097168 | tf_op jit(solution)/shard_map/all_gather | solution.py:77
  543.9 4.0 reshape.23
  547.9 0.0 all-to-all-done.2
  547.9 0.2 maximum_bitcast_fusion
  548.1 0.0 copy-start.3
  548.1 0.0 copy-start.4
  548.1 1.2 copy.10
  549.3 0.0 copy-done.3
  549.3 0.0 copy-done.4
  549.3 1.9 convolution_convert_fusion
  551.2 2.3 reshape.20
  553.5 5.9 %convolution_convert_fusion.1 = bf16[1024,1024]{1,0:T(8,128)(2,1)} fusion(bf16[1024,1024]{1,0:T(8,128)(2,1)} %reshape.20, bf16[1024,1024]{1,0:T(8,128)(2,1)} %reshape.23), kind=kOutput, calls=%fused_computation.7 | convolution fusion | flops 2148532224 | bytes 6291456 | tf_op jit(solution)/shard_map/dot_general | solution.py:75
  (2 shorter events, 0.0 us)
Async XLA Ops:
  6.5 30.0 %copy-start.2 = (f32[8]{0:T(128)S(1)}, f32[8]{0:T(128)}, u32[]{:S(2)}) copy-start(f32[8]{0:T(128)} %param.10) | copy-start | bytes 100
  6.5 30.7 %copy-start.1 = (f32[2048]{0:T(1024)S(1)}, f32[2048]{0:T(1024)}, u32[]{:S(2)}) copy-start(f32[2048]{0:T(1024)} %param.9) | copy-start | bytes 24580
  6.5 118.8 %all-gather.4.cloned.1.call-start = ((), (), s32[]{:S(2)}) async-start(), calls=%async_computation.3 | async-start | bytes 4718592 | tf_op jit(solution)/shard_map/all_gather | solution.py:62
  35.8 508.1 %all-gather.6.cloned.1.call-start = ((), (), s32[]{:S(2)}) async-start(), calls=%async_computation.4 | async-start | bytes 2105344 | tf_op jit(solution)/shard_map/all_gather | solution.py:77
  125.4 3.5 copy-start
  154.8 393.1 %all-to-all-start.2 = ((bf16[8,1,64,1024]{3,2,1,0:T(8,128)(2,1)}), bf16[8,1,64,1024]{3,2,1,0:T(8,128)(2,1)S(1)}, u32[]{:S(2)}, u32[]{:S(2)}) async-start(bf16[8,1,64,1024]{3,2,1,0:T(8,128)(2,1)} %get-tuple-element.6), calls=%async_computation.2 | async-start | bytes 2097152 | tf_op jit(solution)/shard_map/all_to_all | solution.py:45
  548.1 1.2 copy-start.3
  548.1 1.2 copy-start.4
Sparse Core Ops, SparseCore 0:
  35.9 89.4 all-gather.3
  127.3 416.5 all-gather.5
where the time goes:
time: 567 us; the launch traced here: 566 us
  waiting for transfers between devices  472 us (83%)
  blocking collectives  47.4 us (8%)
  between operations  13.5 us (2%)
  matrix products  12.5 us (2%)
  local copies, waits for them, and re-layouts  11.1 us (2%)
    all_gather x1, waiting for transfers between devices, shards(): lax.all_gather(coulomb, ('tm', 'pts'), axis=0, tiled=True)  384 us
    all_gather x1, waiting for transfers between devices, shards(): lax.all_gather(grouped, 'tm', axis=0, tiled=True).astype(jnp.float32)  87.4 us
    all_to_all x1, blocking collectives, sent_to_all(): return lax.all_to_all(copies, axis, split_axis=0, concat_axis=0, tiled=True)  27.3 us
    all_to_all x1, blocking collectives, several_exchanges(): lax.all_to_all(section, axis, split_axis=0, concat_axis=0, tiled=True)  20 us
  transfers between devices with their start and end apart: 3, of which 2 were waited for; matrix products, arithmetic and copies ran while one was open for 3% of the time, Pallas kernels for 0%

commit v1 on v0

--- a/solution.py
+++ b/solution.py
@@ -7,6 +7,18 @@
 PANEL = 1024
 TAU_DEV = 1
 FREQS = 8
+
+
+def turns_replace(inputs):
+    return jnp.concatenate(
+        jax.lax.all_to_all(
+            jnp.stack([inputs for _ in range(jax.lax.axis_size("tm"))]),
+            split_axis=0,
+            concat_axis=0,
+            axis_name="tm",
+        ),
+        axis=0,
+    )
 
 
 def laid_out(pieces, dim):
@@ -59,7 +71,7 @@
     occ_rows = orbitals[:, :NOCC]
     vir_rows = orbitals[:, NOCC:]
     grouped = gather_directly(panel_orbitals, "pts", 0)
-    widened = lax.all_gather(grouped, "tm", axis=0, tiled=True).astype(jnp.float32)
+    widened = turns_replace(grouped).astype(jnp.float32)
     scaled = (widened * decay[0][None, :]).astype(jnp.bfloat16)
     green_occ = contract(occ_rows, scaled[:, :NOCC])
     green_vir = contract(vir_rows, scaled[:, NOCC:])

time: 567 us -> 507 us (0.89)
  waiting for transfers between devices: 472 us -> 407 us
    all_gather x1 -> x0, waiting for transfers between devices: 87.4 us -> none  [shards(): lax.all_gather(grouped, 'tm', axis=0, tiled=True).astype(jnp.float32)]
    all_to_all x0 -> x1, waiting for transfers between devices: none -> 54.8 us  [turns_replace(): jax.lax.all_to_all(jnp.stack([inputs for _ in range(jax.lax.axis_size('tm...]
    all_gather x1, waiting for transfers between devices: 384 us -> 352 us  [shards(): lax.all_gather(coulomb, ('tm', 'pts'), axis=0, tiled=True)]
where the time goes in v1:
time: 507 us; the launch traced here: 506 us
  waiting for transfers between devices  407 us (80%)
  blocking collectives  45.9 us (9%)
  between operations  13.5 us (3%)
  local copies, waits for them, and re-layouts  12.8 us (3%)
  matrix products  12.5 us (2%)
  starting transfers between devices  10 us (2%)
    all_gather x1, waiting for transfers between devices, shards(): lax.all_gather(coulomb, ('tm', 'pts'), axis=0, tiled=True)  352 us
    all_to_all x1, waiting for transfers between devices, turns_replace(): jax.lax.all_to_all(jnp.stack([inputs for _ in range(jax.lax.axis_size('tm...  54.8 us
    all_to_all x1, blocking collectives, sent_to_all(): return lax.all_to_all(copies, axis, split_axis=0, concat_axis=0, tiled=True)  27.3 us
    all_to_all x1, blocking collectives, several_exchanges(): lax.all_to_all(section, axis, split_axis=0, concat_axis=0, tiled=True)  18.5 us
  transfers between devices with their start and end apart: 3, of which 2 were waited for; matrix products, arithmetic and copies ran while one was open for 3% of the time, Pallas kernels for 0%

profile of v1, /device:TPU:98, one launch (start us, length us, event | category | flops | bytes accessed | tf_op | source)
XLA Modules:
  0.0 506.4 jit_solution(2199915234871344978)
XLA Ops:
  6.5 0.9 broadcast_in_dim.2
  7.5 27.3 %all_to_all.20 = bf16[32,4,2048]{2,1,0:T(4,128)(2,1)S(1)} all-to-all(bf16[32,4,2048]{2,1,0:T(4,128)(2,1)S(1)} %broadcast_in_dim.2), channel_id=1, replica_groups=mesh['tm'=8,'pts'=32] {'pts'}, dimensions={0} | all-to-all | bytes 1048576 | tf_op jit(solution)/shard_map/all_to_all | solution.py:32
  34.8 0.1 stack_reshape.2
  34.9 2.5 stack.3
  37.5 0.0 copy-start.2
  37.5 0.0 copy-start.1
  37.5 5.1 %all-to-all-start.1 = ((bf16[8,128,2048]{2,1,0:T(8,128)(2,1)}), bf16[8,128,2048]{2,1,0:T(8,128)(2,1)}, u32[]{:S(2)}, u32[]{:S(2)}) async-start(bf16[8,128,2048]{2,1,0:T(8,128)(2,1)} %stack.3), calls=%async_computation.1 | async-start | bytes 8388608 | tf_op jit(solution)/shard_map/all_to_all | solution.py:14
  42.6 0.0 all-gather.3.cloned.1.call-start
  42.6 0.7 all-gather.3.cloned.1.call-update
  43.3 0.0 copy-done.2
  43.3 0.6 dynamic_slice.3
  43.9 0.0 copy-done.1
  43.9 0.7 multiply_exponential_fusion
  44.6 54.8 %all-to-all-done.1 = bf16[8,128,2048]{2,1,0:T(8,128)(2,1)} async-done(((bf16[8,128,2048]{2,1,0:T(8,128)(2,1)}), bf16[8,128,2048]{2,1,0:T(8,128)(2,1)}, u32[]{:S(2)}, u32[]{:S(2)}) %all-to-all-start.1) | async-done | bytes 4194336 | tf_op jit(solution)/shard_map/all_to_all | solution.py:14
  99.4 0.0 copy-start
  99.4 3.4 fusion
  102.8 0.0 copy-done
  102.8 3.5 fusion.1
  106.3 1.3 negate_convert_fusion
  107.6 1.2 fusion.12
  108.8 18.5 %all_to_all.21 = bf16[8,1,64,1024]{3,2,1,0:T(8,128)(2,1)S(1)} all-to-all(bf16[8,1,64,1024]{3,2,1,0:T(8,128)(2,1)S(1)} %get-tuple-element.5), channel_id=1, replica_groups=mesh['tm'=8,'pts'=32] {'tm'}, dimensions={0} | all-to-all | bytes 2097152 | tf_op jit(solution)/shard_map/all_to_all | solution.py:57
  127.3 4.9 all-to-all-start.3
  132.3 351.9 %all-gather.3.cloned.1.call-done = bf16[256,4,1024]{2,1,0:T(4,128)(2,1)} async-done(((bf16[1,4,1024]{2,1,0:T(4,128)(2,1)}), bf16[256,4,1024]{2,1,0:T(4,128)(2,1)}) %all-gather.3.cloned.1.call-update) | async-done | bytes 2097168 | tf_op jit(solution)/shard_map/all_gather | solution.py:89
  484.1 4.0 reshape.25
  488.1 0.0 all-to-all-done.3
  488.1 0.2 maximum_bitcast_fusion
  488.4 1.2 copy.10
  489.5 0.0 copy-done.3
  489.5 0.0 copy-done.4
  489.5 1.9 convolution_convert_fusion
  491.4 2.3 reshape.21
  493.7 5.9 %convolution_convert_fusion.1 = bf16[1024,1024]{1,0:T(8,128)(2,1)} fusion(bf16[1024,1024]{1,0:T(8,128)(2,1)} %reshape.21, bf16[1024,1024]{1,0:T(8,128)(2,1)} %reshape.25), kind=kOutput, calls=%fused_computation.8 | convolution fusion | flops 2148532224 | bytes 6291456 | tf_op jit(solution)/shard_map/dot_general | solution.py:87
  (2 shorter events, 0.0 us)
Async XLA Ops:
  37.5 5.8 %copy-start.2 = (f32[8]{0:T(128)S(1)}, f32[8]{0:T(128)}, u32[]{:S(2)}) copy-start(f32[8]{0:T(128)} %param.10) | copy-start | bytes 100
  37.5 6.4 %copy-start.1 = (f32[2048]{0:T(1024)S(1)}, f32[2048]{0:T(1024)}, u32[]{:S(2)}) copy-start(f32[2048]{0:T(1024)} %param.9) | copy-start | bytes 24580
  37.5 61.9 %all-to-all-start.1 = ((bf16[8,128,2048]{2,1,0:T(8,128)(2,1)}), bf16[8,128,2048]{2,1,0:T(8,128)(2,1)}, u32[]{:S(2)}, u32[]{:S(2)}) async-start(bf16[8,128,2048]{2,1,0:T(8,128)(2,1)} %stack.3), calls=%async_computation.1 | async-start | bytes 8388608 | tf_op jit(solution)/shard_map/all_to_all | solution.py:14
  42.6 441.6 %all-gather.3.cloned.1.call-start = ((), (), s32[]{:S(2)}) async-start(), calls=%async_computation.4 | async-start | bytes 2105344 | tf_op jit(solution)/shard_map/all_gather | solution.py:89
  99.4 3.5 copy-start
  127.3 360.8 %all-to-all-start.3 = ((bf16[8,1,64,1024]{3,2,1,0:T(8,128)(2,1)}), bf16[8,1,64,1024]{3,2,1,0:T(8,128)(2,1)S(1)}, u32[]{:S(2)}, u32[]{:S(2)}) async-start(bf16[8,1,64,1024]{3,2,1,0:T(8,128)(2,1)} %get-tuple-element.6), calls=%async_computation.3 | async-start | bytes 2097152 | tf_op jit(solution)/shard_map/all_to_all | solution.py:57
  488.1 1.4 copy-start.3
  488.1 1.4 copy-start.4
Sparse Core Ops, SparseCore 0:
  45.3 438.8 all-gather.2
